TPU v7x, 256 devices: a whole 4x4x8 slice. The times are simulated.
256 devices in a mesh: own: 2 (over y_hi), space: 128 (over z, x, y_lo, core).
Axes of the slice: x: 4, y: 4 (y_hi: 2, y_lo: 2; y = y_hi * 2 + y_lo), z: 8, core: 2. Of those that a mesh axis runs over, the one named last changes fastest.
Arguments:
- density: bfloat16 [256, 4, 512, 128], P(None, 'own', 'space'), may hold values from -6 to 6
- cotangent: bfloat16 [256, 4, 512, 128], P(None, 'own', 'space'), may hold values from -6 to 6
- pw_one: bfloat16 [256, 256], P('own'), may hold values from -0.375 to 0.375
- pw_two: bfloat16 [256, 256], P('own'), may hold values from -0.375 to 0.375
- dw_one: bfloat16 [27, 256], P(None, 'own'), may hold values from -1.25 to 1.25
- dw_two: bfloat16 [27, 256], P(None, 'own'), may hold values from -1.25 to 1.25
Outputs:
- grad_input: bfloat16 [256, 4, 512, 128], P(None, 'own', 'space')
- grad_pw_one: float32 [256, 256], P('own')
- grad_pw_two: float32 [256, 256], P('own')
- grad_dw_one: float32 [27, 256], P(None, 'own')
- grad_dw_two: float32 [27, 256], P(None, 'own')
All inputs are finite; a program needn't handle non-finite values.
Results may differ from a plain program's by a relative error of at most 0.01.
Values may be sent and summed in bfloat16 or wider, within the bound.
A program may use at most 192 MiB of HBM per device.

v0:
```python
import math
import jax
import jax.numpy as jnp
from jax import lax
from jax.sharding import PartitionSpec as P

TAP_LIST = [
    (9 * (a + 1) + 3 * (b + 1) + (d + 1), a, b, d)
    for a in (-1, 0, 1)
    for b in (-1, 0, 1)
    for d in (-1, 0, 1)
]


def extended(value, sides, width):
    for axis, dim in sides:
        size, length = (lax.axis_size(axis), value.shape[dim])
        up = [(i, (i + 1) % size) for i in range(size)]
        down = [(j, i) for i, j in up]
        last = lax.slice_in_dim(value, length - width, length, axis=dim)
        first = lax.slice_in_dim(value, 0, width, axis=dim)
        before = lax.ppermute(last, axis, up)
        after = lax.ppermute(first, axis, down)
        value = jnp.concatenate([before, value, after], axis=dim)
    return value


def depthwise(padded, weights, extent_x, extent_y, direction):
    running = jnp.zeros((padded.shape[0], extent_x, extent_y, padded.shape[3]), jnp.float32)
    for k, a, b, d in TAP_LIST:
        start_x = 1 + direction * a
        start_y = 1 + direction * b
        shifted = padded[:, start_x : start_x + extent_x, start_y : start_y + extent_y, :]
        shifted = jnp.roll(shifted, -direction * d, axis=3).astype(jnp.float32)
        running = running + weights[k].astype(jnp.float32)[:, None, None, None] * shifted
    return running


def tap_sums(padded, gradient):
    extent_x = gradient.shape[1]
    extent_y = gradient.shape[2]
    grad_float = gradient.astype(jnp.float32)
    columns = []
    for k, a, b, d in TAP_LIST:
        shifted = padded[:, 1 + a : 1 + a + extent_x, 1 + b : 1 + b + extent_y, :]
        shifted = jnp.roll(shifted, -d, axis=3).astype(jnp.float32)
        columns.append(jnp.sum(shifted * grad_float, axis=(1, 2, 3)))
    return jnp.stack(columns, axis=0)


def pointwise(weights, source):
    layout = source.shape
    flattened = source.reshape(layout[0], -1)
    return jnp.dot(weights.T, flattened, preferred_element_type=jnp.float32).reshape(layout)


def backmap(weights, source):
    layout = source.shape
    flattened = source.reshape(layout[0], -1)
    return jnp.dot(weights, flattened, preferred_element_type=jnp.float32).reshape(layout)


def contract_cells(left, right):
    channels = left.shape[0]
    return lax.dot_general(
        left.reshape(channels, -1),
        right.reshape(channels, -1),
        (((1,), (1,)), ((), ())),
        preferred_element_type=jnp.float32,
    )


def shards(density, cotangent, pw_one, pw_two, dw_one, dw_two):
    channels, extent_x, extent_y, extent_z = density.shape
    weight_one, weight_two, taps_one, taps_two = (
        lax.all_gather(pw_one, "own", axis=0, tiled=True),
        lax.all_gather(pw_two, "own", axis=0, tiled=True),
        lax.all_gather(dw_one, "own", axis=1, tiled=True),
        lax.all_gather(dw_two, "own", axis=1, tiled=True),
    )
    rim_width = 1
    wide_input = extended(density, (("own", 1), ("space", 2)), rim_width)
    first = depthwise(wide_input, taps_one, extent_x, extent_y, 1).astype(jnp.bfloat16)
    pre = pointwise(weight_one, first)
    act = jax.nn.silu(pre).astype(jnp.bfloat16)
    act_padded = extended(act, (("own", 1), ("space", 2)), 1)
    second = depthwise(act_padded, taps_two, extent_x, extent_y, 1).astype(jnp.bfloat16)
    grad_second = backmap(weight_two, cotangent).astype(jnp.bfloat16)
    second_padded = extended(grad_second, (("own", 1), ("space", 2)), 1)
    sigma = jax.nn.sigmoid(pre)
    grad_pre = (
        depthwise(second_padded, taps_two, extent_x, extent_y, -1)
        * (sigma * (1.0 + pre * (1.0 - sigma)))
    ).astype(jnp.bfloat16)
    grad_first = backmap(weight_one, grad_pre).astype(jnp.bfloat16)
    first_padded = extended(grad_first, (("own", 1), ("space", 2)), 1)
    grad_input = (
        cotangent.astype(jnp.float32) + depthwise(first_padded, taps_one, extent_x, extent_y, -1)
    ).astype(jnp.bfloat16)
    total_cells = extent_x * extent_y * extent_z * lax.axis_size("own") * lax.axis_size("space")
    grad_scale = 1.0 / math.sqrt(float(total_cells))
    local_pw_one = contract_cells(first, grad_pre) * grad_scale
    local_pw_two = contract_cells(second, cotangent) * grad_scale
    local_dw_one = tap_sums(wide_input, grad_first) * grad_scale
    local_dw_two = tap_sums(act_padded, grad_second) * grad_scale
    partials = (local_pw_one, local_pw_two, local_dw_one, local_dw_two)
    summed = lax.psum((partials[0], partials[1], partials[2], partials[3]), ("own", "space"))
    share_rows = channels // lax.axis_size("own")
    position = lax.axis_index("own") * share_rows
    result = (
        lax.dynamic_slice_in_dim(summed[0], position, share_rows, 0),
        lax.dynamic_slice_in_dim(summed[1], position, share_rows, 0),
        lax.dynamic_slice_in_dim(summed[2], position, share_rows, 1),
        lax.dynamic_slice_in_dim(summed[3], position, share_rows, 1),
    )
    return (grad_input, result[0], result[1], result[2], result[3])


def solution(mesh):
    in_specs = (
        P(None, "own", "space", None),
        P(None, "own", "space", None),
        P("own", None),
        P("own", None),
        P(None, "own"),
        P(None, "own"),
    )
    out_specs = (
        P(None, "own", "space", None),
        P("own", None),
        P("own", None),
        P(None, "own"),
        P(None, "own"),
    )
    return jax.shard_map(shards, mesh=mesh, in_specs=in_specs, out_specs=out_specs, check_vma=False)
```

profile of v0, /device:TPU:1, one launch (start us, length us, event | category | flops | bytes accessed | tf_op | source)
XLA Modules:
  0.0 458.6 jit_solution(16944286519748687142)
XLA Ops:
  7.3 1.4 copy.90
  8.7 3.8 collective-permute-start.5
  12.6 11.0 %all_gather.12 = bf16[27,256]{1,0:T(8,128)(2,1)S(1)} all-gather(bf16[27,128]{1,0:T(8,128)(2,1)S(1)} %copy-done.80), channel_id=1, replica_groups=mesh['own'=2,'space'=128] {'own'}, dimensions={1}, use_global_device_ids=true | all-gather | bytes 20736 | tf_op jit(solution)/shard_map/all_gather | solution.py:78
  23.6 0.7 slice_convert_fusion.53
  24.9 5.3 %all_gather.13 = bf16[27,256]{1,0:T(8,128)(2,1)S(1)} all-gather(bf16[27,128]{1,0:T(8,128)(2,1)S(1)} %copy-done.81), channel_id=1, replica_groups=mesh['own'=2,'space'=128] {'own'}, dimensions={1}, use_global_device_ids=true | all-gather | bytes 20736 | tf_op jit(solution)/shard_map/all_gather | solution.py:79
  30.2 0.7 slice_convert_fusion.52
  31.5 5.3 %all_gather.15 = bf16[256,256]{1,0:T(8,128)(2,1)S(1)} all-gather(bf16[128,256]{1,0:T(8,128)(2,1)S(1)} %copy-done.24), channel_id=1, replica_groups=mesh['own'=2,'space'=128] {'own'}, dimensions={0}, use_global_device_ids=true | all-gather | bytes 196608 | tf_op jit(solution)/shard_map/all_gather | solution.py:76
  37.2 1.1 copy.88
  38.3 1.0 copy.89
  39.3 5.4 %all_gather.14 = bf16[256,256]{1,0:T(8,128)(2,1)} all-gather(bf16[128,256]{1,0:T(8,128)(2,1)S(1)} %copy-done.25), channel_id=1, replica_groups=mesh['own'=2,'space'=128] {'own'}, dimensions={0}, use_global_device_ids=true | all-gather | bytes 196608 | tf_op jit(solution)/shard_map/all_gather | solution.py:77
  45.0 6.1 %collective-permute-start.6 = (bf16[256,4,1,128]{3,0,2,1:T(8,128)(2,1)S(1)}, bf16[256,4,1,128]{3,0,2,1:T(8,128)(2,1)}, u32[]{:S(2)}, u32[]{:S(2)}) collective-permute-start(bf16[256,4,1,128]{3,0,2,1:T(8,128)(2,1)S(1)} %copy.93), channel_id=1, source_target_pairs={{0,1},{1,2},{2,3},{3,4},{4,5},{5,6},{6,7},{7,8},{8,9},{9,10},{10,1... | collective-permute-start | bytes 786440 | tf_op jit(solution)/shard_map/ppermute | solution.py:22
  51.1 0.9 copy.96
  52.0 1.4 fusion.146
  53.4 2.3 fusion.217
  55.8 1.8 copy.94
  57.6 3.4 collective-permute-done.7
  60.9 1.8 copy.97
  62.7 1.2 maximum_maximum_fusion.1
  64.3 1.8 fusion.289
  66.4 11.0 %add_convert_fusion = (bf16[256,2,4,128]{0,3,2,1:T(8,128)(2,1)S(1)}, f32[256,2,4,128]{0,3,2,1:T(8,128)}, f32[256,2,4,128]{0,3,2,1:T(8,128)}, f32[256,2,4,128]{0,...) fusion(bf16[256,2,4,128]{0,3,2,1:T(8,128)(2,1)S(1)} %copy.90, ...), kind=kLoop, calls=%fused_computation.272 | loop fusion | flops 57933824 | bytes 27225088 | tf_op jit(solution)/shard_map/convert_element_type | solution.py:83
  78.7 2.6 collective-permute-start.13
  81.3 0.8 collective-permute-start.12
  82.1 1.5 maximum_convert_fusion
  83.7 2.8 collective-permute-done.13
  86.5 5.6 %collective-permute-done.12 = bf16[256,1,4,128]{0,3,2,1:T(8,128)(2,1)S(1)} collective-permute-done((bf16[256,1,4,128]{0,3,2,1:T(8,128)(2,1)S(1)}, bf16[256,1,4,128]{0,3,2,1:T(8,128)(2,1)S(1)}, u32[]{:S(2)}, u32[]{:S(2)}) %collective-permute-start.12) | collective-permute-done | bytes 262176 | tf_op jit(solution)/shard_map/ppermute | solution.py:22
  92.2 1.5 collective-permute-start.14
  93.7 1.0 collective-permute-start.15
  95.2 1.8 collective-permute-done.14
  97.1 2.5 collective-permute-done.15
  99.8 0.7 fusion.284
  100.8 2.1 fusion.120
  103.0 0.8 fusion.294
  103.8 2.9 collective-permute-start
  106.8 0.7 fusion.283
  107.5 1.4 fusion.135
  108.8 1.3 fusion.131
  110.4 2.1 fusion.136
  112.7 5.8 %fusion = f32[256,256]{1,0:T(8,128)} fusion(bf16[256,2,4,128]{0,3,2,1:T(8,128)(2,1)S(1)} %copy-done.11, bf16[256,2,4,128]{0,3,2,1:T(8,128)(2,1)S(1)} %multiply_convert_fusion, f32[256]{0:T(256)S(1)} %bitcast.317, f32[256]{0:T(256)S(1)} %bitcast.319, f32[256]{0:T(256)S(1)} %bitcast.321, f32[256]{0:T(256)S(1)} %bitcast.323, f32[256]{0:T(256)S(1)} %bitcast.325, ...), kind=kOutput, calls=%fused_computation.119 | convolution fusion | flops 192217088 | bytes 14986240 | tf_op jit(solution)/shard_map/dot_general | solution.py:65
  118.5 1.2 fusion.137
  119.7 5.2 %stack.223 = f32[27,256]{1,0:T(8,128)} concatenate(f32[1,256]{1,0:T(1,128)} %bitcast.379, f32[1,256]{1,0:T(1,128)} %bitcast.306, f32[1,256]{1,0:T(1,128)} %bitcast.380, f32[1,256]{1,0:T(1,128)} %bitcast.309, f32[1,256]{1,0:T(1,128)} %bitcast.381, f32[1,256]{1,0:T(1,128)} %bitcast.310, f32[1,256]{1,0:T(1,128)S(1)} %bitcast.275, f32[1,256]{1,0:T(1,128)} %bitcast.303, ...), dimensions={0} | concatenate | bytes 55296 | tf_op jit(solution)/shard_map/stack | solution.py:48
  125.0 1.4 broadcast_multiply_fusion
  126.4 3.4 collective-permute-start.3
  129.8 2.6 collective-permute-start.2
  132.9 3.0 collective-permute-done.3
  136.2 0.7 fusion.288
  137.2 0.7 fusion.287
  138.4 9.1 %fusion.139 = bf16[256,2,4,128]{0,3,2,1:T(8,128)(2,1)S(1)} fusion(f32[256,2,4,128]{0,3,2,1:T(8,128)S(1)} %bitcast.215, bf16[256,2,4,128]{0,3,2,1:T(8,128)(2,1)S(1)} %get-tuple-element.274, bf16[256,1,4,128]{0,3,2,1:T(8,128)(2,1)S(1)} %collective-permute-done, bf16[256,1,4,128]{0,3,2,1:T(8,128)(2,1)S(1)} %collective-permute-done.1, ...), kind=kLoop, calls=%fused_computation.274 | loop fusion | flops 58982400 | bytes 14666752 | tf_op jit(solution)/shard_map/convert_element_type | solution.py:94
  147.5 0.8 copy-done.17
  148.3 1.1 fusion.1
  149.4 8.2 %fusion.95 = (f32[256]{0:T(256)S(1)}, f32[256]{0:T(256)S(1)}, f32[256]{0:T(256)S(1)}, f32[256]{0:T(256)S(1)}, f32[256]{0:T(256)}, /*index=5*/f32[256]{0:T(256)},...) fusion(f32[256,2,4,128]{0,3,2,1:T(8,128)} %get-tuple-element.96, ...), kind=kOutput, calls=%fused_computation.227 | convolution fusion | flops 144174592 | bytes 20072448 | tf_op jit(solution)/shard_map/dot_general | solution.py:60
  157.6 0.8 fusion.293
  158.4 2.9 collective-permute-start.8
  161.5 2.3 fusion.77
  164.1 87.9 %all-reduce = (f32[27,256]{1,0:T(8,128)S(1)}, f32[27,256]{1,0:T(8,128)S(1)}) all-reduce(f32[27,256]{1,0:T(8,128)S(1)} %broadcast_multiply_fusion.1, f32[27,256]{1,0:T(8,128)S(1)} %copy-done.23), channel_id=1, replica_groups=mesh['own'=2,'space'=128] {'own','space'}, use_global_device_ids=true, to_apply=%region_29.30 | all-reduce | flops 13824 | bytes 110592 | tf_op jit(solution)/shard_map/psum | solution.py:107
  253.2 168.2 %all-reduce.4.cloned.1.call-done = (f32[256,256]{1,0:T(8,128)}, f32[256,256]{1,0:T(8,128)}) async-done(((f32[256,256]{1,0:T(8,128)}, f32[256,256]{1,0:T(8,128)}), (f32[256,256]{1,0:T(8,128)}, f32[256,256]{1,0:T(8,128)})) %all-reduce.4.cloned.1.call-update) | async-done | bytes 524304 | tf_op jit(solution)/shard_map/psum | solution.py:107
  421.4 1.6 constant_dynamic-slice_fusion.3
  423.0 1.6 constant_dynamic-slice_fusion.2
  424.8 3.3 collective-permute-start.11
  428.6 1.6 fusion.152
  430.2 1.2 collective-permute-done.11
  431.5 5.6 %collective-permute-done.10 = bf16[256,4,1,128]{3,0,2,1:T(8,128)(2,1)S(1)} collective-permute-done((bf16[256,4,1,128]{3,0,2,1:T(8,128)(2,1)S(1)}, bf16[256,4,1,128]{3,0,2,1:T(8,128)(2,1)S(1)}, u32[]{:S(2)}, u32[]{:S(2)}) %collective-permute-start.10) | collective-permute-done | bytes 262176 | tf_op jit(solution)/shard_map/ppermute | solution.py:23
  438.4 0.7 fusion.285
  440.0 9.5 %fusion.138 = bf16[256,2,4,128]{0,3,2,1:T(8,128)(2,1)} fusion(bf16[256,2,4,128]{0,3,2,1:T(8,128)(2,1)S(1)} %bitcast.213, bf16[256,2,4,128]{0,3,2,1:T(8,128)(2,1)S(1)} %copy-done.12, bf16[256,1,4,128]{0,3,2,1:T(8,128)(2,1)S(1)} %collective-permute-done.8, bf16[256,1,4,128]{0,3,2,1:T(8,128)(2,1)S(1)} %collective-permute-done.9, ...), kind=kLoop, calls=%fused_computation.273 | loop fusion | flops 57409536 | bytes 14142464 | tf_op jit(solution)/shard_map/convert_element_type | solution.py:99
  449.5 2.1 copy.112
  (344 shorter events, 9.9 us)
Async XLA Ops:
  7.2 5.4 %copy-start.80 = (bf16[27,128]{1,0:T(8,128)(2,1)S(1)}, bf16[27,128]{1,0:T(8,128)(2,1)}, u32[]{:S(2)}) copy-start(bf16[27,128]{1,0:T(8,128)(2,1)} %param.10) | copy-start | bytes 20740
  7.2 17.7 %copy-start.81 = (bf16[27,128]{1,0:T(8,128)(2,1)S(1)}, bf16[27,128]{1,0:T(8,128)(2,1)}, u32[]{:S(2)}) copy-start(bf16[27,128]{1,0:T(8,128)(2,1)} %param.11) | copy-start | bytes 20740
  7.2 24.3 %copy-start.24 = (bf16[128,256]{1,0:T(8,128)(2,1)S(1)}, bf16[128,256]{1,0:T(8,128)(2,1)}, u32[]{:S(2)}) copy-start(bf16[128,256]{1,0:T(8,128)(2,1)} %param.8) | copy-start | bytes 196612
  7.2 29.6 %copy-start.18 = (bf16[256,2,4,128]{3,2,1,0:T(4,128)(2,1)S(1)}, bf16[256,2,4,128]{3,2,1,0:T(4,128)(2,1)}, u32[]{:S(2)}) copy-start(bf16[256,2,4,128]{3,2,1,0:T(4,128)(2,1)} %param.7) | copy-start | bytes 1572868
  7.2 414.2 %all-reduce.4.cloned.1.call-start = ((), (), s32[]{:S(2)}) async-start(), calls=%async_computation | async-start | bytes 1048576 | tf_op jit(solution)/shard_map/psum | solution.py:107
  8.7 36.1 %collective-permute-start.5 = (bf16[256,1,4,128]{0,3,2,1:T(8,128)(2,1)S(1)}, bf16[256,1,4,128]{0,3,2,1:T(8,128)(2,1)S(1)}, u32[]{:S(2)}, u32[]{:S(2)}) collective-permute-start(bf16[256,1,4,128]{0,3,2,1:T(8,128)(2,1)S(1)} %get-tuple-element.218), channel_id=1, source_target_pairs={{128,0},{0,128},{129,1},{1,129},{130,2},{2,130},{131,3},{3,131},{1... | collective-permute-start | bytes 786440 | tf_op jit(solution)/shard_map/ppermute | solution.py:23
  12.5 32.3 %collective-permute-start.4 = (bf16[256,1,4,128]{0,3,2,1:T(8,128)(2,1)S(1)}, bf16[256,1,4,128]{0,3,2,1:T(8,128)(2,1)S(1)}, u32[]{:S(2)}, u32[]{:S(2)}) collective-permute-start(bf16[256,1,4,128]{0,3,2,1:T(8,128)(2,1)S(1)} %get-tuple-element.217), channel_id=1, source_target_pairs={{0,128},{128,0},{1,129},{129,1},{2,130},{130,2},{3,131},{131,3},{4... | collective-permute-start | bytes 786440 | tf_op jit(solution)/shard_map/ppermute | solution.py:22
  45.0 10.7 %collective-permute-start.6 = (bf16[256,4,1,128]{3,0,2,1:T(8,128)(2,1)S(1)}, bf16[256,4,1,128]{3,0,2,1:T(8,128)(2,1)}, u32[]{:S(2)}, u32[]{:S(2)}) collective-permute-start(bf16[256,4,1,128]{3,0,2,1:T(8,128)(2,1)S(1)} %copy.93), channel_id=1, source_target_pairs={{0,1},{1,2},{2,3},{3,4},{4,5},{5,6},{6,7},{7,8},{8,9},{9,10},{10,1... | collective-permute-start | bytes 786440 | tf_op jit(solution)/shard_map/ppermute | solution.py:22
  52.0 8.9 %collective-permute-start.7 = (bf16[256,4,1,128]{3,0,2,1:T(8,128)(2,1)}, bf16[256,4,1,128]{3,0,2,1:T(8,128)(2,1)}, u32[]{:S(2)}, u32[]{:S(2)}) collective-permute-start(bf16[256,4,1,128]{3,0,2,1:T(8,128)(2,1)} %copy.96), channel_id=1, source_target_pairs={{1,0},{2,1},{3,2},{4,3},{5,4},{6,5},{7,6},{8,7},{9,8},{10,9},{11,1... | collective-permute-start | bytes 786440 | tf_op jit(solution)/shard_map/ppermute | solution.py:23
  53.4 2.3 copy-start.3
  53.4 2.3 copy-start.5
  78.7 7.8 %collective-permute-start.13 = (bf16[256,1,4,128]{0,3,2,1:T(8,128)(2,1)S(1)}, bf16[256,1,4,128]{0,3,2,1:T(8,128)(2,1)S(1)}, u32[]{:S(2)}, u32[]{:S(2)}) collective-permute-start(bf16[256,1,4,128]{0,3,2,1:T(8,128)(2,1)S(1)} %get-tuple-element.190), channel_id=1, source_target_pairs={{128,0},{0,128},{129,1},{1,129},{130,2},{2,130},{131,3},{3,131},{1... | collective-permute-start | bytes 786440 | tf_op jit(solution)/shard_map/ppermute | solution.py:23
  81.3 10.8 %collective-permute-start.12 = (bf16[256,1,4,128]{0,3,2,1:T(8,128)(2,1)S(1)}, bf16[256,1,4,128]{0,3,2,1:T(8,128)(2,1)S(1)}, u32[]{:S(2)}, u32[]{:S(2)}) collective-permute-start(bf16[256,1,4,128]{0,3,2,1:T(8,128)(2,1)S(1)} %get-tuple-element.189), channel_id=1, source_target_pairs={{0,128},{128,0},{1,129},{129,1},{2,130},{130,2},{3,131},{131,3},{4... | collective-permute-start | bytes 786440 | tf_op jit(solution)/shard_map/ppermute | solution.py:22
  92.2 4.9 %collective-permute-start.14 = (bf16[256,4,1,128]{0,3,2,1:T(8,128)(2,1)S(1)}, bf16[256,4,1,128]{0,3,2,1:T(8,128)(2,1)S(1)}, u32[]{:S(2)}, u32[]{:S(2)}) collective-permute-start(bf16[256,4,1,128]{0,3,2,1:T(8,128)(2,1)S(1)} %get-tuple-element.147), channel_id=1, source_target_pairs={{0,1},{1,2},{2,3},{3,4},{4,5},{5,6},{6,7},{7,8},{8,9},{9,10},{10,1... | collective-permute-start | bytes 786440 | tf_op jit(solution)/shard_map/ppermute | solution.py:22
  93.7 5.8 %collective-permute-start.15 = (bf16[256,4,1,128]{0,3,2,1:T(8,128)(2,1)S(1)}, bf16[256,4,1,128]{0,3,2,1:T(8,128)(2,1)S(1)}, u32[]{:S(2)}, u32[]{:S(2)}) collective-permute-start(bf16[256,4,1,128]{0,3,2,1:T(8,128)(2,1)S(1)} %get-tuple-element.148), channel_id=1, source_target_pairs={{1,0},{2,1},{3,2},{4,3},{5,4},{6,5},{7,6},{8,7},{9,8},{10,9},{11,1... | collective-permute-start | bytes 786440 | tf_op jit(solution)/shard_map/ppermute | solution.py:23
  103.8 22.5 %collective-permute-start = (bf16[256,1,4,128]{0,3,2,1:T(8,128)(2,1)}, bf16[256,1,4,128]{0,3,2,1:T(8,128)(2,1)S(1)}, u32[]{:S(2)}, u32[]{:S(2)}) collective-permute-start(bf16[256,1,4,128]{0,3,2,1:T(8,128)(2,1)} %get-tuple-element.210), channel_id=1, source_target_pairs={{0,128},{128,0},{1,129},{129,1},{2,130},{130,2},{3,131},{131,3},{4... | collective-permute-start | bytes 786440 | tf_op jit(solution)/shard_map/ppermute | solution.py:22
  106.7 19.6 %collective-permute-start.1 = (bf16[256,1,4,128]{0,3,2,1:T(8,128)(2,1)}, bf16[256,1,4,128]{0,3,2,1:T(8,128)(2,1)S(1)}, u32[]{:S(2)}, u32[]{:S(2)}) collective-permute-start(bf16[256,1,4,128]{0,3,2,1:T(8,128)(2,1)} %get-tuple-element.209), channel_id=1, source_target_pairs={{128,0},{0,128},{129,1},{1,129},{130,2},{2,130},{131,3},{3,131},{1... | collective-permute-start | bytes 786440 | tf_op jit(solution)/shard_map/ppermute | solution.py:23
  110.1 2.3 copy-start.100
  110.1 2.3 copy-start.102
  110.2 2.3 copy-start.104
  110.2 2.3 copy-start.106
  110.2 2.3 copy-start.108
  110.2 2.3 copy-start.110
  110.2 2.3 copy-start.112
  110.2 2.3 copy-start.114
  110.2 2.3 copy-start.116
  110.2 2.3 copy-start.118
  110.2 2.3 copy-start.120
  110.2 2.3 copy-start.122
  110.3 2.3 copy-start.124
  110.3 2.3 copy-start.126
  110.3 2.3 copy-start.128
  110.3 2.3 copy-start.130
  110.3 2.3 copy-start.132
  110.3 2.3 copy-start.134
  110.3 2.3 copy-start.136
  110.3 2.3 copy-start.138
  110.3 2.3 copy-start.140
  110.3 2.3 copy-start.142
  110.4 2.3 copy-start.144
  110.4 2.3 copy-start.146
  110.4 2.3 copy-start.148
  126.4 9.6 %collective-permute-start.3 = (bf16[256,4,1,128]{0,3,2,1:T(8,128)(2,1)S(1)}, bf16[256,4,1,128]{0,3,2,1:T(8,128)(2,1)S(1)}, u32[]{:S(2)}, u32[]{:S(2)}) collective-permute-start(bf16[256,4,1,128]{0,3,2,1:T(8,128)(2,1)S(1)} %get-tuple-element.156), channel_id=1, source_target_pairs={{0,1},{1,2},{2,3},{3,4},{4,5},{5,6},{6,7},{7,8},{8,9},{9,10},{10,1... | collective-permute-start | bytes 786440 | tf_op jit(solution)/shard_map/ppermute | solution.py:22
  129.8 6.1 %collective-permute-start.2 = (bf16[256,4,1,128]{0,3,2,1:T(8,128)(2,1)S(1)}, bf16[256,4,1,128]{0,3,2,1:T(8,128)(2,1)S(1)}, u32[]{:S(2)}, u32[]{:S(2)}) collective-permute-start(bf16[256,4,1,128]{0,3,2,1:T(8,128)(2,1)S(1)} %get-tuple-element.155), channel_id=1, source_target_pairs={{1,0},{2,1},{3,2},{4,3},{5,4},{6,5},{7,6},{8,7},{9,8},{10,9},{11,1... | collective-permute-start | bytes 786440 | tf_op jit(solution)/shard_map/ppermute | solution.py:23
  138.4 9.9 %copy-start.20 = (bf16[256,2,4,128]{0,3,2,1:T(8,128)(2,1)S(1)}, bf16[256,2,4,128]{0,3,2,1:T(8,128)(2,1)}, u32[]{:S(2)}) copy-start(bf16[256,2,4,128]{0,3,2,1:T(8,128)(2,1)} %copy-done.19) | copy-start | bytes 1572868
  158.4 266.2 %collective-permute-start.8 = (bf16[256,1,4,128]{0,3,2,1:T(8,128)(2,1)}, bf16[256,1,4,128]{0,3,2,1:T(8,128)(2,1)S(1)}, u32[]{:S(2)}, u32[]{:S(2)}) collective-permute-start(bf16[256,1,4,128]{0,3,2,1:T(8,128)(2,1)} %get-tuple-element.200), channel_id=1, source_target_pairs={{0,128},{128,0},{1,129},{129,1},{2,130},{130,2},{3,131},{131,3},{4... | collective-permute-start | bytes 786440 | tf_op jit(solution)/shard_map/ppermute | solution.py:22
  161.3 263.2 %collective-permute-start.9 = (bf16[256,1,4,128]{0,3,2,1:T(8,128)(2,1)}, bf16[256,1,4,128]{0,3,2,1:T(8,128)(2,1)S(1)}, u32[]{:S(2)}, u32[]{:S(2)}) collective-permute-start(bf16[256,1,4,128]{0,3,2,1:T(8,128)(2,1)} %get-tuple-element.199), channel_id=1, source_target_pairs={{128,0},{0,128},{129,1},{1,129},{130,2},{2,130},{131,3},{3,131},{1... | collective-permute-start | bytes 786440 | tf_op jit(solution)/shard_map/ppermute | solution.py:23
  161.4 2.4 copy-start.82
  161.4 2.4 copy-start.83
  161.4 2.4 copy-start.84
  161.4 2.4 copy-start.85
  161.4 2.4 copy-start.86
  161.4 2.4 copy-start.87
  161.4 2.4 copy-start.88
  161.5 2.4 copy-start.89
  161.5 2.4 copy-start.90
  161.5 2.4 copy-start.91
  161.5 2.4 copy-start.92
  161.5 2.4 copy-start.93
  161.5 2.4 copy-start.94
  161.5 2.4 copy-start.95
  161.5 2.5 copy-start.23
  424.8 6.6 %collective-permute-start.11 = (bf16[256,4,1,128]{3,0,2,1:T(8,128)(2,1)S(1)}, bf16[256,4,1,128]{3,0,2,1:T(8,128)(2,1)S(1)}, u32[]{:S(2)}, u32[]{:S(2)}) collective-permute-start(bf16[256,4,1,128]{3,0,2,1:T(8,128)(2,1)S(1)} %copy.106), channel_id=1, source_target_pairs={{0,1},{1,2},{2,3},{3,4},{4,5},{5,6},{6,7},{7,8},{8,9},{9,10},{10,1... | collective-permute-start | bytes 786440 | tf_op jit(solution)/shard_map/ppermute | solution.py:22
  428.2 8.9 %collective-permute-start.10 = (bf16[256,4,1,128]{3,0,2,1:T(8,128)(2,1)S(1)}, bf16[256,4,1,128]{3,0,2,1:T(8,128)(2,1)S(1)}, u32[]{:S(2)}, u32[]{:S(2)}) collective-permute-start(bf16[256,4,1,128]{3,0,2,1:T(8,128)(2,1)S(1)} %copy.104), channel_id=1, source_target_pairs={{1,0},{2,1},{3,2},{4,3},{5,4},{6,5},{7,6},{8,7},{9,8},{10,9},{11,1... | collective-permute-start | bytes 786440 | tf_op jit(solution)/shard_map/ppermute | solution.py:23
  (103 other events, 170.5 us)
Sparse Core Ops, SparseCore 0:
  161.5 259.8 all-reduce.3
where the time goes:
time: 468 us; the launch traced here: 459 us
  waiting for transfers between devices  194 us (41%)
  blocking collectives  115 us (25%)
  other arithmetic  52.1 us (11%)
  local copies, waits for them, and re-layouts  31.8 us (7%)
  starting transfers between devices  31.6 us (7%)
  matrix products  17.5 us (4%)
  between operations  16.6 us (4%)
    psum x1, waiting for transfers between devices, shards(): lax.psum((partials[0], partials[1], partials[2], partials[3]), ('own', 's...  168 us
    psum x1, blocking collectives, shards(): lax.psum((partials[0], partials[1], partials[2], partials[3]), ('own', 's...  87.9 us
    ppermute x8, starting transfers between devices, extended(): before = lax.ppermute(last, axis, up)  21.1 us
    ppermute x8, waiting for transfers between devices, extended(): after = lax.ppermute(first, axis, down)  14.3 us
    ppermute x8, waiting for transfers between devices, extended(): before = lax.ppermute(last, axis, up)  11.7 us
    convert_element_type x1, other arithmetic, shards(): depthwise(wide_input, taps_one, extent_x, extent_y, 1).astype(jnp.bfloat16)  11 us
    all_gather x1, blocking collectives, shards(): lax.all_gather(dw_one, 'own', axis=1, tiled=True)  11 us
    ppermute x8, starting transfers between devices, extended(): after = lax.ppermute(first, axis, down)  10.5 us
  transfers between devices with their start and end apart: 17, of which 9 were waited for; matrix products, arithmetic and copies ran while one was open for 9% of the time, Pallas kernels for 0%

commit v1 on v0

--- a/solution.py
+++ b/solution.py
@@ -104,7 +104,9 @@
     local_dw_one = tap_sums(wide_input, grad_first) * grad_scale
     local_dw_two = tap_sums(act_padded, grad_second) * grad_scale
     partials = (local_pw_one, local_pw_two, local_dw_one, local_dw_two)
-    summed = lax.psum((partials[0], partials[1], partials[2], partials[3]), ("own", "space"))
+    summed = lax.psum(
+        lax.psum((partials[0], partials[1], partials[2], partials[3]), "own"), "space"
+    )
     share_rows = channels // lax.axis_size("own")
     position = lax.axis_index("own") * share_rows
     result = (

time: 468 us -> 1770 us (3.78)
  waiting for transfers between devices: 194 us -> 1010 us
  blocking collectives: 115 us -> 593 us
    psum x1 -> x2, waiting for transfers between devices: 168 us -> 993 us  [the longest x1 993 us: shards(): lax.psum(lax.psum((partials[0], partials[1], partials[2], partials[3]), '...]
    psum x1 -> x2, blocking collectives: 87.9 us -> 566 us  [the longest x1 555 us: shards(): lax.psum(lax.psum((partials[0], partials[1], partials[2], partials[3]), '...]
  transfers between devices with their start and end apart: 17 -> 18, of which waited for: 9 -> 7; matrix products, arithmetic and copies ran while one was open for 9% -> 3% of each run, Pallas kernels for 0% -> 0%
where the time goes in v1:
time: 1770 us; the launch traced here: 1760 us
  waiting for transfers between devices  1010 us (57%)
  blocking collectives  593 us (34%)
  other arithmetic  53.8 us (3%)
  local copies, waits for them, and re-layouts  35.4 us (2%)
  starting transfers between devices  35.1 us (2%)
    psum x1, waiting for transfers between devices, shards(): lax.psum(lax.psum((partials[0], partials[1], partials[2], partials[3]), '...  993 us
    psum x1, blocking collectives, shards(): lax.psum(lax.psum((partials[0], partials[1], partials[2], partials[3]), '...  555 us
  transfers between devices with their start and end apart: 18, of which 7 were waited for; matrix products, arithmetic and copies ran while one was open for 3% of the time, Pallas kernels for 0%

profile of v1, /device:TPU:1, one launch (start us, length us, event | category | flops | bytes accessed | tf_op | source)
XLA Modules:
  0.0 1763.1 jit_solution(17184221709993477015)
XLA Ops:
  7.3 1.4 copy.90
  8.7 3.8 collective-permute-start.5
  12.6 11.0 all_gather.12
  24.9 5.4 all_gather.13
  31.5 5.3 all_gather.15
  37.2 1.1 copy.88
  38.3 1.0 copy.89
  39.3 5.4 all_gather.14
  45.0 6.1 collective-permute-start.6
  51.1 0.8 copy.96
  52.0 1.4 fusion.146
  53.4 2.3 fusion.217
  55.7 1.8 copy.94
  57.5 3.4 collective-permute-done.7
  60.9 1.8 copy.97
  62.7 1.2 maximum_maximum_fusion.1
  64.3 1.8 fusion.289
  66.4 11.0 add_convert_fusion
  78.7 2.6 collective-permute-start.13
  81.3 0.8 collective-permute-start.12
  82.1 1.6 maximum_convert_fusion
  83.7 2.9 collective-permute-done.13
  86.5 5.6 collective-permute-done.12
  92.2 1.5 collective-permute-start.14
  93.7 1.0 collective-permute-start.15
  95.2 1.8 collective-permute-done.14
  97.0 2.5 collective-permute-done.15
  100.8 2.2 fusion.120
  103.0 0.8 fusion.294
  103.8 2.9 collective-permute-start
  107.5 1.4 fusion.135
  108.9 1.3 fusion.131
  110.4 2.1 fusion.136
  112.7 5.8 fusion
  118.5 1.2 fusion.137
  119.7 5.3 stack.223
  125.0 1.4 broadcast_multiply_fusion
  126.4 3.4 collective-permute-start.3
  129.9 2.6 collective-permute-start.2
  132.9 3.0 collective-permute-done.3
  136.2 0.7 fusion.288
  137.2 0.7 fusion.287
  138.4 9.1 fusion.139
  147.5 0.8 copy-done.14
  148.3 1.0 fusion.1
  149.4 8.3 fusion.95
  157.6 0.8 fusion.293
  158.5 2.9 collective-permute-start.8
  161.6 0.9 fusion.77
  162.9 10.7 all-reduce.2
  173.5 555.1 %all-reduce = (f32[27,256]{1,0:T(8,128)S(1)}, f32[27,256]{1,0:T(8,128)S(1)}) all-reduce(f32[27,256]{1,0:T(8,128)S(1)} %get-tuple-element.84, f32[27,256]{1,0:T(8,128)S(1)} %get-tuple-element.85), channel_id=1, replica_groups=mesh['own'=2,'space'=128] {'space'}, use_global_device_ids=true, to_apply=%region_32.33 | all-reduce | flops 13824 | bytes 110592 | tf_op jit(solution)/shard_map/psum | solution.py:107
  730.1 1.8 collective-permute-start.11
  732.1 5.2 collective-permute-start.10
  737.3 1.6 fusion.152
  738.9 0.9 copy.107
  739.7 0.9 copy.105
  740.6 1.4 pad_maximum_fusion.2
  742.0 2.0 fusion.286
  744.3 2.1 fusion.285
  746.6 11.5 fusion.138
  758.1 2.1 copy.112
  760.2 992.7 %all-reduce.7.cloned.1.call-done = (f32[256,256]{1,0:T(8,128)}, f32[256,256]{1,0:T(8,128)}) async-done(((f32[256,256]{1,0:T(8,128)}, f32[256,256]{1,0:T(8,128)}), (f32[256,256]{1,0:T(8,128)}, f32[256,256]{1,0:T(8,128)})) %all-reduce.7.cloned.1.call-update) | async-done | bytes 524304 | tf_op jit(solution)/shard_map/psum | solution.py:107
  1752.9 1.6 constant_dynamic-slice_fusion.3
  1754.5 1.6 constant_dynamic-slice_fusion.2
  (336 shorter events, 10.8 us)
Async XLA Ops:
  7.2 5.4 copy-start.74
  7.2 17.7 %copy-start.75 = (bf16[27,128]{1,0:T(8,128)(2,1)S(1)}, bf16[27,128]{1,0:T(8,128)(2,1)}, u32[]{:S(2)}) copy-start(bf16[27,128]{1,0:T(8,128)(2,1)} %param.11) | copy-start | bytes 20740
  7.2 24.3 %copy-start.21 = (bf16[128,256]{1,0:T(8,128)(2,1)S(1)}, bf16[128,256]{1,0:T(8,128)(2,1)}, u32[]{:S(2)}) copy-start(bf16[128,256]{1,0:T(8,128)(2,1)} %param.8) | copy-start | bytes 196612
  7.2 29.6 %copy-start.15 = (bf16[256,2,4,128]{3,2,1,0:T(4,128)(2,1)S(1)}, bf16[256,2,4,128]{3,2,1,0:T(4,128)(2,1)}, u32[]{:S(2)}) copy-start(bf16[256,2,4,128]{3,2,1,0:T(4,128)(2,1)} %param.7) | copy-start | bytes 1572868
  7.2 739.1 %all-reduce.9.cloned.1.call-start = ((), (), s32[]{:S(2)}) async-start(), calls=%async_computation.1 | async-start | bytes 1048576 | tf_op jit(solution)/shard_map/psum | solution.py:108
  8.7 36.1 %collective-permute-start.5 = (bf16[256,1,4,128]{0,3,2,1:T(8,128)(2,1)S(1)}, bf16[256,1,4,128]{0,3,2,1:T(8,128)(2,1)S(1)}, u32[]{:S(2)}, u32[]{:S(2)}) collective-permute-start(bf16[256,1,4,128]{0,3,2,1:T(8,128)(2,1)S(1)} %get-tuple-element.222), channel_id=1, source_target_pairs={{128,0},{0,128},{129,1},{1,129},{130,2},{2,130},{131,3},{3,131},{1... | collective-permute-start | bytes 786440 | tf_op jit(solution)/shard_map/ppermute | solution.py:23
  12.5 32.3 %collective-permute-start.4 = (bf16[256,1,4,128]{0,3,2,1:T(8,128)(2,1)S(1)}, bf16[256,1,4,128]{0,3,2,1:T(8,128)(2,1)S(1)}, u32[]{:S(2)}, u32[]{:S(2)}) collective-permute-start(bf16[256,1,4,128]{0,3,2,1:T(8,128)(2,1)S(1)} %get-tuple-element.221), channel_id=1, source_target_pairs={{0,128},{128,0},{1,129},{129,1},{2,130},{130,2},{3,131},{131,3},{4... | collective-permute-start | bytes 786440 | tf_op jit(solution)/shard_map/ppermute | solution.py:22
  45.0 10.7 collective-permute-start.6
  52.0 8.9 collective-permute-start.7
  53.4 2.3 copy-start.5
  53.4 2.3 copy-start.7
  78.7 7.8 collective-permute-start.13
  81.3 10.8 collective-permute-start.12
  92.2 4.8 collective-permute-start.14
  93.7 5.8 collective-permute-start.15
  103.8 22.6 %collective-permute-start = (bf16[256,1,4,128]{0,3,2,1:T(8,128)(2,1)}, bf16[256,1,4,128]{0,3,2,1:T(8,128)(2,1)S(1)}, u32[]{:S(2)}, u32[]{:S(2)}) collective-permute-start(bf16[256,1,4,128]{0,3,2,1:T(8,128)(2,1)} %get-tuple-element.214), channel_id=1, source_target_pairs={{0,128},{128,0},{1,129},{129,1},{2,130},{130,2},{3,131},{131,3},{4... | collective-permute-start | bytes 786440 | tf_op jit(solution)/shard_map/ppermute | solution.py:22
  106.7 19.7 %collective-permute-start.1 = (bf16[256,1,4,128]{0,3,2,1:T(8,128)(2,1)}, bf16[256,1,4,128]{0,3,2,1:T(8,128)(2,1)S(1)}, u32[]{:S(2)}, u32[]{:S(2)}) collective-permute-start(bf16[256,1,4,128]{0,3,2,1:T(8,128)(2,1)} %get-tuple-element.213), channel_id=1, source_target_pairs={{128,0},{0,128},{129,1},{1,129},{130,2},{2,130},{131,3},{3,131},{1... | collective-permute-start | bytes 786440 | tf_op jit(solution)/shard_map/ppermute | solution.py:23
  110.2 2.3 copy-start.98
  110.2 2.3 copy-start.100
  110.2 2.3 copy-start.102
  110.2 2.3 copy-start.104
  110.2 2.3 copy-start.106
  110.2 2.3 copy-start.108
  110.2 2.3 copy-start.110
  110.2 2.3 copy-start.112
  110.3 2.3 copy-start.114
  110.3 2.3 copy-start.116
  110.3 2.3 copy-start.118
  110.3 2.3 copy-start.120
  110.3 2.3 copy-start.122
  126.4 9.6 collective-permute-start.3
  129.9 6.1 collective-permute-start.2
  138.4 9.9 copy-start.17
  149.4 12.3 copy-start.1
  158.5 571.4 %collective-permute-start.8 = (bf16[256,1,4,128]{0,3,2,1:T(8,128)(2,1)}, bf16[256,1,4,128]{0,3,2,1:T(8,128)(2,1)S(1)}, u32[]{:S(2)}, u32[]{:S(2)}) collective-permute-start(bf16[256,1,4,128]{0,3,2,1:T(8,128)(2,1)} %get-tuple-element.204), channel_id=1, source_target_pairs={{0,128},{128,0},{1,129},{129,1},{2,130},{130,2},{3,131},{131,3},{4... | collective-permute-start | bytes 786440 | tf_op jit(solution)/shard_map/ppermute | solution.py:22
  161.5 568.4 %collective-permute-start.9 = (bf16[256,1,4,128]{0,3,2,1:T(8,128)(2,1)}, bf16[256,1,4,128]{0,3,2,1:T(8,128)(2,1)S(1)}, u32[]{:S(2)}, u32[]{:S(2)}) collective-permute-start(bf16[256,1,4,128]{0,3,2,1:T(8,128)(2,1)} %get-tuple-element.203), channel_id=1, source_target_pairs={{128,0},{0,128},{129,1},{1,129},{130,2},{2,130},{131,3},{3,131},{1... | collective-permute-start | bytes 786440 | tf_op jit(solution)/shard_map/ppermute | solution.py:23
  162.8 1590.1 %all-reduce.7.cloned.1.call-start = ((), (), s32[]{:S(2)}) async-start(), calls=%async_computation | async-start | bytes 1048576 | tf_op jit(solution)/shard_map/psum | solution.py:107
  729.9 9.0 copy-start.4
  730.1 8.7 collective-permute-start.11
  732.1 7.7 collective-permute-start.10
  744.1 2.3 copy-start.24
  744.1 2.3 copy-start.26
  744.1 2.3 copy-start.28
  744.1 2.3 copy-start.30
  744.1 2.4 copy-start.32
  744.1 2.4 copy-start.34
  744.1 2.4 copy-start.36
  744.1 2.4 copy-start.38
  744.1 2.4 copy-start.40
  744.1 2.4 copy-start.42
  744.1 2.4 copy-start.44
  744.1 2.4 copy-start.46
  744.1 2.4 copy-start.48
  744.2 2.4 copy-start.50
  744.2 2.4 copy-start.52
  744.2 2.4 copy-start.54
  744.2 2.4 copy-start.56
  744.2 2.4 copy-start.58
  744.2 2.4 copy-start.60
  744.2 2.4 copy-start.62
  744.2 2.4 copy-start.64
  744.2 2.4 copy-start.66
  744.2 2.4 copy-start.68
  744.3 2.4 copy-start.70
  (98 other events, 165.8 us)
Sparse Core Ops, SparseCore 0:
  162.9 50.6 all-reduce.8
  746.5 1006.3 all-reduce.6
